TPU v7x, 32 devices: a whole 2x2x4 slice. The times are simulated.
32 devices in a mesh: grp: 2 (over y), seg: 16 (over z, x, core).
Axes of the slice: x: 2, y: 2, z: 4, core: 2. Of those that a mesh axis runs over, the one named last changes fastest.
Arguments:
- strain: bfloat16 [524288], P(('grp', 'seg')), parts along dimension 0, may hold values from -6 to 6
- templates: bfloat16 [128, 512], P('seg'), may hold values from -6 to 6
Outputs:
- profile: float32 [32, 128], P(('grp', 'seg')), parts along dimension 0
- overall: float32 [256], P('grp'), parts along dimension 0
There are 2 independent parts, one for each index of `grp`. A program takes and returns all parts, laid end to end along the dimension named above; an argument that names none is the same for every part. Nothing has to cross between parts.
All inputs are finite; a program needn't handle non-finite values.
Results may differ from a plain program's by a relative error of at most 0.0003.
Values may be sent and summed in bfloat16 or wider, within the bound.
A program may use at most 256 MiB of HBM per device.

v0:
```python
import jax
import jax.numpy as jnp
from jax import lax
from jax.sharding import PartitionSpec as P

EPSILON = 1e-05


def passed_along(block, axis, distance):
    devices = range(lax.axis_size(axis))
    route = [(i - distance, i) for i in devices if i - distance in devices]
    return lax.ppermute(block, axis, route)


def hankel(extended, width):
    count = (extended.shape[0] - width) // width
    lower = extended[: count * width].reshape(count, width)
    upper = extended[width:].reshape(count, width)
    paired = jnp.concatenate([lower, upper], axis=1)
    tiled = jnp.tile(paired, (1, width + 1))[:, : width * (2 * width + 1)]
    windows = tiled.reshape(count, width, 2 * width + 1)[:, :, :width].reshape(count * width, width)
    return (paired, windows)


def window_stats(paired, width):
    rows = jnp.arange(2 * width)[:, None]
    cols = jnp.arange(width)[None, :]
    ones_band = ((rows >= cols) & (rows < cols + width)).astype(jnp.float32)
    floats = paired.astype(jnp.float32)
    totals = jnp.dot(floats, ones_band, precision=lax.Precision.HIGHEST).reshape(-1)
    squared = jnp.dot(floats * floats, ones_band, precision=lax.Precision.HIGHEST).reshape(-1)
    win_mean = totals / width
    variance = squared / width - win_mean * win_mean
    return (win_mean, jnp.sqrt(jnp.maximum(variance, 0.0) + EPSILON))


def template_minima(windows, win_mean, win_dev, usable, templates):
    width = templates.shape[1]
    floats = templates.astype(jnp.float32)
    t_mean = jnp.mean(floats, axis=1)
    t_dev = jnp.sqrt(jnp.mean((floats - t_mean[:, None]) ** 2, axis=1) + EPSILON)
    products = lax.dot_general(
        windows, templates, (((1,), (1,)), ((), ())), preferred_element_type=jnp.float32
    )
    rho = (products - width * win_mean[:, None] * t_mean[None, :]) / (
        width * win_dev[:, None] * t_dev[None, :]
    )
    distance = jnp.sqrt(jnp.maximum(2.0 - 2.0 * rho, 0.0))
    distance = jnp.where(usable[:, None], distance, jnp.inf)
    return jnp.min(distance, axis=0)


def per_device(strain, templates):
    width = templates.shape[1]
    seg_len = strain.shape[0]
    following = passed_along(strain[:width], "seg", -1)
    extended = jnp.concatenate([strain, following])
    paired, windows = hankel(extended, width)
    win_mean, win_dev = window_stats(paired, width)
    number = lax.axis_index("seg")
    places = number * seg_len + jnp.arange(seg_len, dtype=jnp.int32)
    usable = places <= seg_len * lax.axis_size("seg") - width
    gathered = lax.all_gather(templates, "seg", axis=0, tiled=True)
    minima = template_minima(windows, win_mean, win_dev, usable, gathered)
    profile = minima[None, :]
    collected = lax.all_gather(profile, "seg", axis=0, tiled=True)
    overall = jnp.min(collected, axis=0)
    return (profile, overall)


def solution(mesh):
    in_specs = (P(("grp", "seg")), P("seg", None))
    out_specs = (P(("grp", "seg"), None), P("grp"))
    return jax.shard_map(
        per_device, mesh=mesh, in_specs=in_specs, out_specs=out_specs, check_vma=False
    )
```

profile of v0, /device:TPU:0, one launch (start us, length us, event | category | flops | bytes accessed | tf_op | source)
XLA Modules:
  0.0 228.7 jit_solution(16680242244528655759)
XLA Ops:
  0.6 0.7 slice.22
  1.3 1.3 collective-permute-start
  2.6 0.8 reshape.71
  3.4 24.3 %all_gather.6 = bf16[128,512]{1,0:T(8,128)(2,1)S(1)} all-gather(bf16[8,512]{1,0:T(8,128)(2,1)} %param.3), channel_id=1, replica_groups=mesh['grp'=2,'seg'=16] {'seg'}, dimensions={0}, use_global_device_ids=true | all-gather | bytes 139264 | tf_op jit(solution)/shard_map/all_gather | solution.py:63
  27.7 0.1 convert_reduce_fusion
  27.9 0.2 fusion.24
  28.1 0.0 collective-permute-done
  28.1 0.8 pad_maximum_fusion
  28.9 0.5 fusion.12
  29.4 0.8 fusion.18
  30.3 11.3 %tile.4 = bf16[32,513,1024]{2,1,0:T(8,128)(2,1)} broadcast(bf16[32,1024]{1,0:T(8,128)(2,1)S(1)} %constant_dynamic-update-slice_fusion), dimensions={0,2} | broadcast | bytes 33685504 | tf_op jit(solution)/shard_map/tile | solution.py:20
  41.5 23.4 %copy.4 = bf16[4,8,513,1024]{3,1,2,0:T(8,128)(2,1)} copy(bf16[4,8,513,1024]{3,2,1,0:T(8,128)(2,1)} %bitcast.14) | data formatting | bytes 67239936
  64.9 22.9 %slice.27 = bf16[32,524800]{1,0:T(8,128)(2,1)} slice(bf16[32,525312]{1,0:T(8,128)(2,1)} %bitcast.15), slice={[0:32], [0:524800]} | slice | bytes 67174400 | tf_op jit(solution)/shard_map/slice | solution.py:20
  87.8 108.4 %reshape.72 = bf16[32,512,1025]{2,1,0:T(8,128)(2,1)} reshape(bf16[32,524800]{1,0:T(8,128)(2,1)} %slice.27) | data formatting | bytes 67174400 | tf_op jit(solution)/shard_map/reshape | solution.py:21
  196.2 0.0 slice-start
  196.3 5.7 %slice-done = bf16[32,512,512]{2,1,0:T(8,128)(2,1)S(1)} async-done(((bf16[32,512,1025]{2,1,0:T(8,128)(2,1)}), bf16[32,512,512]{2,1,0:T(8,128)(2,1)S(1)}, s32[]{:S(2)}) %slice-start) | async-done | bytes 16777240 | tf_op jit(solution)/shard_map/slice | solution.py:21
  202.0 8.7 %fusion.7 = f32[128]{0:T(128)S(1)} fusion(f32[128]{0:T(128)S(1)} %add_sqrt_fusion, f32[16384]{0:T(1024)S(1)} %sqrt_multiply_fusion, f32[128]{0:T(128)S(1)} %broadcast_multiply_fusion, f32[16384]{0:T(1024)S(1)} %bitcast.18, bf16[16384,512]{1,0:T(8,128)(2,1)S(1)} %bitcast.16, bf16[128,512]{1,0:T(8,128)(2,1)S(1)} %all_gather.6, ...), kind=kOutput, calls=%fused_computation.10 | convolution fusion | flops 2166358016 | bytes 17057280 | tf_op jit(solution)/shard_map/dot_general | solution.py:42
  210.7 0.0 copy-start
  210.7 17.4 %all-gather.1 = f32[16,1,128]{2,1,0:T(1,128)S(1)} all-gather(f32[1,1,128]{2,1,0:T(1,128)S(1)} %bitcast.20), channel_id=2, replica_groups=mesh['grp'=2,'seg'=16] {'seg'}, dimensions={0}, use_global_device_ids=true | all-gather | bytes 8704 | tf_op jit(solution)/shard_map/all_gather | solution.py:66
  228.2 0.5 reduce_min.19
  228.7 0.0 copy-done
  (10 shorter events, 0.1 us)
Async XLA Ops:
  1.3 26.8 %collective-permute-start = (bf16[512]{0:T(512)(128)(2,1)S(1)}, bf16[512]{0:T(512)(128)(2,1)S(1)}, u32[]{:S(2)}, u32[]{:S(2)}) collective-permute-start(bf16[512]{0:T(512)(128)(2,1)S(1)} %slice.22), channel_id=1, source_target_pairs={{1,0},{2,1},{3,2},{4,3},{5,4},{6,5},{7,6},{8,7},{9,8},{10,9},{11,1... | collective-permute-start | bytes 3080 | tf_op jit(solution)/shard_map/ppermute | solution.py:12
  196.2 5.8 %slice-start = ((bf16[32,512,1025]{2,1,0:T(8,128)(2,1)}), bf16[32,512,512]{2,1,0:T(8,128)(2,1)S(1)}, s32[]{:S(2)}) async-start(bf16[32,512,1025]{2,1,0:T(8,128)(2,1)} %reshape.72), calls=%async_computation | async-start | bytes 33554432 | tf_op jit(solution)/shard_map/slice | solution.py:21
  210.7 18.0 %copy-start = (f32[128]{0:T(128)}, f32[128]{0:T(128)S(1)}, u32[]{:S(2)}) copy-start(f32[128]{0:T(128)S(1)} %fusion.7) | copy-start | bytes 1540
where the time goes:
time: 229 us
  local copies, waits for them, and re-layouts  173 us (76%)
  blocking collectives  41.8 us (18%)
  matrix products  9.95 us (4%)
    reshape x1, local copies, waits for them, and re-layouts, hankel(): tiled.reshape(count, width, 2 * width + 1)[:, :, :width]  108 us
    all_gather x1, blocking collectives, per_device(): gathered = lax.all_gather(templates, 'seg', axis=0, tiled=True)  24.3 us
    unnamed x6, local copies, waits for them, and re-layouts  23.4 us
    slice x1, local copies, waits for them, and re-layouts, hankel(): tiled = jnp.tile(paired, (1, width + 1))[:, :width * (2 * width + 1)]  22.9 us
    all_gather x1, blocking collectives, per_device(): collected = lax.all_gather(profile, 'seg', axis=0, tiled=True)  17.4 us
    another operation x1, local copies, waits for them, and re-layouts, hankel(): tiled = jnp.tile(paired, (1, width + 1))[:, :width * (2 * width + 1)]  11.3 us
    dot_general x1, matrix products, template_minima(): lax.dot_general(windows, templates, (((1,), (1,)), ((), ())), preferred_e...  8.69 us
    slice x2, local copies, waits for them, and re-layouts, hankel(): tiled.reshape(count, width, 2 * width + 1)[:, :, :width]  5.73 us
  transfers between devices with their start and end apart: 1, of which 0 were waited for; matrix products, arithmetic and copies ran while one was open for 0% of the time, Pallas kernels for 0%

commit v1 on v0

--- a/solution.py
+++ b/solution.py
@@ -63,7 +63,9 @@
     gathered = lax.all_gather(templates, "seg", axis=0, tiled=True)
     minima = template_minima(windows, win_mean, win_dev, usable, gathered)
     profile = minima[None, :]
-    collected = lax.all_gather(profile, "seg", axis=0, tiled=True)
+    collected = jnp.concatenate(
+        lax.all_to_all(jnp.stack([profile] * lax.axis_size("seg")), "seg", 0, 0), axis=0
+    )
     overall = jnp.min(collected, axis=0)
     return (profile, overall)
 

time: 229 us -> 221 us (0.965)
  blocking collectives: 41.8 us -> 33.3 us
    all_gather x1 -> x0, blocking collectives: 17.4 us -> none  [per_device(): collected = lax.all_gather(profile, 'seg', axis=0, tiled=True)]
    all_to_all x0 -> x1, blocking collectives: none -> 9.01 us  [per_device(): lax.all_to_all(jnp.stack([profile] * lax.axis_size('seg')), 'seg', 0, 0)]
  transfers between devices with their start and end apart: 1 -> 1, of which waited for: 0 -> 0; matrix products, arithmetic and copies ran while one was open for 0% -> 1% of each run, Pallas kernels for 0% -> 0%
where the time goes in v1:
time: 221 us; the launch traced here: 220 us
  local copies, waits for them, and re-layouts  173 us (78%)
  blocking collectives  33.3 us (15%)
  matrix products  9.95 us (5%)
    reshape x1, local copies, waits for them, and re-layouts, hankel(): tiled.reshape(count, width, 2 * width + 1)[:, :, :width]  108 us
    all_gather x1, blocking collectives, per_device(): gathered = lax.all_gather(templates, 'seg', axis=0, tiled=True)  24.3 us
    unnamed x6, local copies, waits for them, and re-layouts  23.4 us
    slice x1, local copies, waits for them, and re-layouts, hankel(): tiled = jnp.tile(paired, (1, width + 1))[:, :width * (2 * width + 1)]  22.9 us
    another operation x1, local copies, waits for them, and re-layouts, hankel(): tiled = jnp.tile(paired, (1, width + 1))[:, :width * (2 * width + 1)]  11.3 us
    all_to_all x1, blocking collectives, per_device(): lax.all_to_all(jnp.stack([profile] * lax.axis_size('seg')), 'seg', 0, 0)  9.01 us
    dot_general x1, matrix products, template_minima(): lax.dot_general(windows, templates, (((1,), (1,)), ((), ())), preferred_e...  8.69 us
    slice x2, local copies, waits for them, and re-layouts, hankel(): tiled.reshape(count, width, 2 * width + 1)[:, :, :width]  5.73 us
  transfers between devices with their start and end apart: 1, of which 0 were waited for; matrix products, arithmetic and copies ran while one was open for 1% of the time, Pallas kernels for 0%

profile of v1, /device:TPU:0, one launch (start us, length us, event | category | flops | bytes accessed | tf_op | source)
XLA Modules:
  0.0 220.3 jit_solution(5956024881237796135)
XLA Ops:
  0.6 0.7 slice.22
  1.3 1.3 collective-permute-start
  2.6 0.8 reshape.74
  3.4 24.3 %all_gather.3 = bf16[128,512]{1,0:T(8,128)(2,1)S(1)} all-gather(bf16[8,512]{1,0:T(8,128)(2,1)} %param.3), channel_id=1, replica_groups=mesh['grp'=2,'seg'=16] {'seg'}, dimensions={0}, use_global_device_ids=true | all-gather | bytes 139264 | tf_op jit(solution)/shard_map/all_gather | solution.py:63
  27.7 0.1 convert_reduce_fusion
  27.9 0.2 fusion.24
  28.1 0.0 collective-permute-done
  28.1 0.8 pad_maximum_fusion
  28.9 0.5 fusion.12
  29.4 0.8 fusion.18
  30.3 11.3 %tile.4 = bf16[32,513,1024]{2,1,0:T(8,128)(2,1)} broadcast(bf16[32,1024]{1,0:T(8,128)(2,1)S(1)} %constant_dynamic-update-slice_fusion), dimensions={0,2} | broadcast | bytes 33685504 | tf_op jit(solution)/shard_map/tile | solution.py:20
  41.5 23.4 %copy.5 = bf16[4,8,513,1024]{3,1,2,0:T(8,128)(2,1)} copy(bf16[4,8,513,1024]{3,2,1,0:T(8,128)(2,1)} %bitcast.14) | data formatting | bytes 67239936
  64.9 22.9 %slice.27 = bf16[32,524800]{1,0:T(8,128)(2,1)} slice(bf16[32,525312]{1,0:T(8,128)(2,1)} %bitcast.15), slice={[0:32], [0:524800]} | slice | bytes 67174400 | tf_op jit(solution)/shard_map/slice | solution.py:20
  87.8 108.4 %reshape.75 = bf16[32,512,1025]{2,1,0:T(8,128)(2,1)} reshape(bf16[32,524800]{1,0:T(8,128)(2,1)} %slice.27) | data formatting | bytes 67174400 | tf_op jit(solution)/shard_map/reshape | solution.py:21
  196.2 0.0 slice-start
  196.3 5.7 %slice-done = bf16[32,512,512]{2,1,0:T(8,128)(2,1)S(1)} async-done(((bf16[32,512,1025]{2,1,0:T(8,128)(2,1)}), bf16[32,512,512]{2,1,0:T(8,128)(2,1)S(1)}, s32[]{:S(2)}) %slice-start) | async-done | bytes 16777240 | tf_op jit(solution)/shard_map/slice | solution.py:21
  202.0 8.7 %fusion.7 = f32[128]{0:T(128)S(1)} fusion(f32[128]{0:T(128)S(1)} %add_sqrt_fusion, f32[16384]{0:T(1024)S(1)} %sqrt_multiply_fusion, f32[128]{0:T(128)S(1)} %broadcast_multiply_fusion, f32[16384]{0:T(1024)S(1)} %bitcast.18, bf16[16384,512]{1,0:T(8,128)(2,1)S(1)} %bitcast.16, bf16[128,512]{1,0:T(8,128)(2,1)S(1)} %all_gather.3, ...), kind=kOutput, calls=%fused_computation.10 | convolution fusion | flops 2166358016 | bytes 17057280 | tf_op jit(solution)/shard_map/dot_general | solution.py:42
  210.7 0.0 copy-start
  210.7 9.0 %all_to_all.5 = f32[16,1,128]{2,1,0:T(1,128)S(1)} all-to-all(f32[16,1,128]{2,1,0:T(1,128)S(1)} %stack.3), channel_id=1, replica_groups=mesh['grp'=2,'seg'=16] {'seg'}, dimensions={0} | all-to-all | bytes 16384 | tf_op jit(solution)/shard_map/all_to_all | solution.py:67
  219.7 0.5 reduce_min.19
  220.3 0.0 copy-done
  (11 shorter events, 0.2 us)
Async XLA Ops:
  1.3 26.8 %collective-permute-start = (bf16[512]{0:T(512)(128)(2,1)S(1)}, bf16[512]{0:T(512)(128)(2,1)S(1)}, u32[]{:S(2)}, u32[]{:S(2)}) collective-permute-start(bf16[512]{0:T(512)(128)(2,1)S(1)} %slice.22), channel_id=1, source_target_pairs={{1,0},{2,1},{3,2},{4,3},{5,4},{6,5},{7,6},{8,7},{9,8},{10,9},{11,1... | collective-permute-start | bytes 3080 | tf_op jit(solution)/shard_map/ppermute | solution.py:12
  196.2 5.8 %slice-start = ((bf16[32,512,1025]{2,1,0:T(8,128)(2,1)}), bf16[32,512,512]{2,1,0:T(8,128)(2,1)S(1)}, s32[]{:S(2)}) async-start(bf16[32,512,1025]{2,1,0:T(8,128)(2,1)} %reshape.75), calls=%async_computation.1 | async-start | bytes 33554432 | tf_op jit(solution)/shard_map/slice | solution.py:21
  210.7 9.6 %copy-start = (f32[128]{0:T(128)}, f32[128]{0:T(128)S(1)}, u32[]{:S(2)}) copy-start(f32[128]{0:T(128)S(1)} %fusion.7) | copy-start | bytes 1540
